TPU v7x, 32 devices: a whole 2x2x4 slice. The times are simulated.
32 devices in a mesh: dp: 8 (over z, core), own: 4 (over y, x).
Axes of the slice: x: 2, y: 2, z: 4, core: 2. Of those that a mesh axis runs over, the one named last changes fastest.
Arguments:
- tokens_in: bfloat16 [64, 256, 768], P(('dp', 'own')), may hold values from -6 to 6
- condition: float32 [64, 768], P(('dp', 'own')), may hold values from -6 to 6
- cotangent: bfloat16 [64, 256, 768], P(('dp', 'own')), may hold values from -6 to 6
- w_qkv: float32 [768, 2304], P('own', 'dp'), may hold values from -0.21875 to 0.21875
- w_proj: float32 [768, 768], P('own', 'dp'), may hold values from -0.625 to 0.625
- w_fc1: float32 [768, 3072], P('own', 'dp'), may hold values from -0.21875 to 0.21875
- w_fc2: float32 [3072, 768], P('dp', 'own'), may hold values from -0.109375 to 0.109375
- w_ada: float32 [768, 4608], P('own', 'dp'), may hold values from -0.21875 to 0.21875
- mom_qkv: float32 [768, 2304], P('own', 'dp'), may hold values from -384 to 384
- mom_proj: float32 [768, 768], P('own', 'dp'), may hold values from -384 to 384
- mom_fc1: float32 [768, 3072], P('own', 'dp'), may hold values from -384 to 384
- mom_fc2: float32 [3072, 768], P('dp', 'own'), may hold values from -384 to 384
- mom_ada: float32 [768, 4608], P('own', 'dp'), may hold values from -384 to 384
- biases: float32 [10752], P(('dp', 'own')), may hold values from -4 to 4
- bias_mom: float32 [10752], P(('dp', 'own')), may hold values from -224 to 224
Outputs:
- block_out: float32 [64, 256, 768], P(('dp', 'own'))
- grad_in: float32 [64, 256, 768], P(('dp', 'own'))
- grad_cond: float32 [64, 768], P(('dp', 'own'))
- grad_qkv: float32 [768, 2304], P('own', 'dp')
- grad_proj: float32 [768, 768], P('own', 'dp')
- grad_fc1: float32 [768, 3072], P('own', 'dp')
- grad_fc2: float32 [3072, 768], P('dp', 'own')
- grad_ada: float32 [768, 4608], P('own', 'dp')
- grad_bias: float32 [10752], P(('dp', 'own'))
- new_qkv: float32 [768, 2304], P('own', 'dp')
- new_proj: float32 [768, 768], P('own', 'dp')
- new_fc1: float32 [768, 3072], P('own', 'dp')
- new_fc2: float32 [3072, 768], P('dp', 'own')
- new_ada: float32 [768, 4608], P('own', 'dp')
- moment_qkv: float32 [768, 2304], P('own', 'dp')
- moment_proj: float32 [768, 768], P('own', 'dp')
- moment_fc1: float32 [768, 3072], P('own', 'dp')
- moment_fc2: float32 [3072, 768], P('dp', 'own')
- moment_ada: float32 [768, 4608], P('own', 'dp')
- new_bias: float32 [10752], P(('dp', 'own'))
- moment_bias: float32 [10752], P(('dp', 'own'))
- moment_norms: float32 [5], replicated
All inputs are finite; a program needn't handle non-finite values.
Results may differ from a plain program's by a relative error of at most 0.028.
Values may be sent and summed in bfloat16 or wider, within the bound.
No kernel may reach another device: no remote copies, remote signals or barrier semaphores. Data moves between devices by JAX's collectives and lax.ppermute only.
A program may use at most 192 MiB of HBM per device.

v0:
```python
import math
import jax
import jax.numpy as jnp
from jax import lax
from jax.sharding import PartitionSpec as P

HEADS = 12
NS_ITERS = 5
momentum_rate = 0.9
learn_rate = 0.15
bias_rate = 0.002
coef_first = 3.4445
coef_second = -4.775
coef_third = 2.0315
gelu_scale = math.sqrt(2.0 / math.pi)
norm_epsilon = 1e-06


def for_sending(array):
    return jax.tree.map(lambda a: a.astype(jnp.bfloat16) if a.dtype == jnp.float32 else a, array)


def batched(form, left, right):
    return jnp.einsum(form, left, right, preferred_element_type=jnp.float32)


def layer_stats(values):
    mean_value = jnp.mean(values, axis=-1, keepdims=True)
    centered = values - mean_value
    inv_std = lax.rsqrt(jnp.mean(centered * centered, axis=-1, keepdims=True) + norm_epsilon)
    return (centered * inv_std, inv_std)


def norm_back(grad_normed, normed, inv_std):
    first = jnp.mean(grad_normed, axis=-1, keepdims=True)
    second = jnp.mean(grad_normed * normed, axis=-1, keepdims=True)
    return inv_std * (grad_normed - first - normed * second)


def gelu_value(inner):
    return 0.5 * inner * (1.0 + jnp.tanh(gelu_scale * (inner + 0.044715 * inner * inner * inner)))


def gelu_slope(inner):
    tangent = jnp.tanh(gelu_scale * (inner + 0.044715 * inner * inner * inner))
    return 0.5 * (1.0 + tangent) + 0.5 * inner * (1.0 - tangent * tangent) * gelu_scale * (
        1.0 + 3.0 * 0.044715 * inner * inner
    )


def block_pass(tokens_in, condition, cotangent, w_qkv, w_proj, w_fc1, w_fc2, w_ada, bias_low):
    latents, length, features = tokens_in.shape
    hidden_units = w_fc1.shape[1]
    head_count = HEADS
    head_size = features // head_count
    score_scale = 1.0 / math.sqrt(head_size)
    row_count = latents * length
    bias_full = bias_low.astype(jnp.float32)
    b_query = bias_full[:features]
    b_value = bias_full[features : 2 * features]
    b_proj = bias_full[2 * features : 3 * features]
    b_fc1 = bias_full[3 * features : 3 * features + hidden_units]
    b_fc2 = bias_full[3 * features + hidden_units : 4 * features + hidden_units]
    b_ada = bias_full[4 * features + hidden_units :]
    cond_act = jax.nn.silu(condition).astype(jnp.bfloat16)
    modulation = jnp.dot(cond_act, w_ada, preferred_element_type=jnp.float32) + b_ada
    pieces = [
        modulation[:, index * features : (index + 1) * features][:, None, :] for index in range(6)
    ]
    shift_one, scale_one, gate_one, shift_two, scale_two, gate_two = pieces
    residual = tokens_in.astype(jnp.float32)
    normed_one, inv_one = layer_stats(residual)
    modulated_one = (normed_one * (1.0 + scale_one) + shift_one).astype(jnp.bfloat16)
    qkv_proj = jnp.dot(
        modulated_one.reshape(row_count, features), w_qkv, preferred_element_type=jnp.float32
    )
    qkv_proj = qkv_proj.reshape(latents, length, 3 * features)
    head_shape = (latents, length, head_count, head_size)
    query_heads = (qkv_proj[..., :features] + b_query).astype(jnp.bfloat16).reshape(head_shape)
    key_heads = qkv_proj[..., features : 2 * features].astype(jnp.bfloat16).reshape(head_shape)
    value_heads = (qkv_proj[..., 2 * features :] + b_value).astype(jnp.bfloat16).reshape(head_shape)
    scores = batched("bqhd,bkhd->bhqk", query_heads, key_heads) * score_scale
    row_max = jnp.max(scores, axis=-1, keepdims=True)
    log_total = row_max + jnp.log(jnp.sum(jnp.exp(scores - row_max), axis=-1, keepdims=True))
    attn_probs = jnp.exp(scores - log_total).astype(jnp.bfloat16)
    attn_out = (
        batched("bhqk,bkhd->bqhd", attn_probs, value_heads)
        .astype(jnp.bfloat16)
        .reshape(row_count, features)
    )
    branch_one = (jnp.dot(attn_out, w_proj, preferred_element_type=jnp.float32) + b_proj).reshape(
        latents, length, features
    )
    middle = residual + gate_one * branch_one
    normed_two, inv_two = layer_stats(middle)
    modulated_two = (
        (normed_two * (1.0 + scale_two) + shift_two)
        .astype(jnp.bfloat16)
        .reshape(row_count, features)
    )
    fc1_pre = jnp.dot(modulated_two, w_fc1, preferred_element_type=jnp.float32) + b_fc1
    fc1_act = gelu_value(fc1_pre).astype(jnp.bfloat16)
    branch_two = (jnp.dot(fc1_act, w_fc2, preferred_element_type=jnp.float32) + b_fc2).reshape(
        latents, length, features
    )
    block_out = middle + gate_two * branch_two
    cot_float = cotangent.astype(jnp.float32)
    d_gate_two = jnp.sum(cot_float * branch_two, axis=1)
    d_branch_two = cot_float * gate_two
    dbranch_low = d_branch_two.astype(jnp.bfloat16).reshape(row_count, features)
    g_fc2 = jnp.dot(fc1_act.T, dbranch_low, preferred_element_type=jnp.float32)
    gb_fc2 = jnp.sum(d_branch_two, axis=(0, 1))
    d_pre = jnp.dot(dbranch_low, w_fc2.T, preferred_element_type=jnp.float32) * gelu_slope(fc1_pre)
    dpre_low = d_pre.astype(jnp.bfloat16)
    g_fc1 = jnp.dot(modulated_two.T, dpre_low, preferred_element_type=jnp.float32)
    gb_fc1 = jnp.sum(d_pre, axis=0)
    d_mod_two = jnp.dot(dpre_low, w_fc1.T, preferred_element_type=jnp.float32).reshape(
        latents, length, features
    )
    d_shift_two = jnp.sum(d_mod_two, axis=1)
    d_scale_two = jnp.sum(d_mod_two * normed_two, axis=1)
    d_middle = cot_float + norm_back(d_mod_two * (1.0 + scale_two), normed_two, inv_two)
    d_gate_one = jnp.sum(d_middle * branch_one, axis=1)
    d_branch_one = d_middle * gate_one
    dbranch_one_low = d_branch_one.astype(jnp.bfloat16).reshape(row_count, features)
    g_proj = jnp.dot(attn_out.T, dbranch_one_low, preferred_element_type=jnp.float32)
    gb_proj = jnp.sum(d_branch_one, axis=(0, 1))
    d_attn = (
        jnp.dot(dbranch_one_low, w_proj.T, preferred_element_type=jnp.float32)
        .astype(jnp.bfloat16)
        .reshape(head_shape)
    )
    scores_again = batched("bqhd,bkhd->bhqk", query_heads, key_heads) * score_scale
    probs_again = jnp.exp(scores_again - log_total)
    d_probs = batched("bqhd,bkhd->bhqk", d_attn, value_heads)
    delta = jnp.sum(probs_again * d_probs, axis=-1, keepdims=True)
    d_scores = (probs_again * (d_probs - delta) * score_scale).astype(jnp.bfloat16)
    d_query = batched("bhqk,bkhd->bqhd", d_scores, key_heads)
    d_key = batched("bhqk,bqhd->bkhd", d_scores, query_heads)
    d_value = batched("bhqk,bqhd->bkhd", probs_again.astype(jnp.bfloat16), d_attn)
    flat_shape = (latents, length, features)
    d_qkv = jnp.concatenate(
        [d_query.reshape(flat_shape), d_key.reshape(flat_shape), d_value.reshape(flat_shape)],
        axis=-1,
    )
    dqkv_low = d_qkv.astype(jnp.bfloat16).reshape(row_count, 3 * features)
    g_qkv = jnp.dot(
        modulated_one.reshape(row_count, features).T, dqkv_low, preferred_element_type=jnp.float32
    )
    gb_query = jnp.sum(d_query, axis=(0, 1)).reshape(features)
    gb_value = jnp.sum(d_value, axis=(0, 1)).reshape(features)
    d_mod_one = jnp.dot(dqkv_low, w_qkv.T, preferred_element_type=jnp.float32).reshape(flat_shape)
    d_shift_one = jnp.sum(d_mod_one, axis=1)
    d_scale_one = jnp.sum(d_mod_one * normed_one, axis=1)
    grad_in = d_middle + norm_back(d_mod_one * (1.0 + scale_one), normed_one, inv_one)
    d_modulation = jnp.concatenate(
        [d_shift_one, d_scale_one, d_gate_one, d_shift_two, d_scale_two, d_gate_two], axis=-1
    )
    dmod_low = d_modulation.astype(jnp.bfloat16)
    g_ada = jnp.dot(cond_act.T, dmod_low, preferred_element_type=jnp.float32)
    gb_ada = jnp.sum(d_modulation, axis=0)
    sigmoid_c = jax.nn.sigmoid(condition)
    grad_cond = jnp.dot(dmod_low, w_ada.T, preferred_element_type=jnp.float32) * (
        sigmoid_c * (1.0 + condition * (1.0 - sigmoid_c))
    )
    grad_bias = jnp.concatenate([gb_query, gb_value, gb_proj, gb_fc1, gb_fc2, gb_ada])
    return (
        block_out,
        grad_in,
        grad_cond,
        (g_qkv, g_proj, g_fc1, g_fc2, g_ada),
        grad_bias,
        cond_act,
        dmod_low,
    )


def per_device(
    tokens_in,
    condition,
    cotangent,
    w_qkv,
    w_proj,
    w_fc1,
    w_fc2,
    w_ada,
    mom_qkv,
    mom_proj,
    mom_fc1,
    mom_fc2,
    mom_ada,
    biases,
    bias_mom,
):
    own_part = (
        lax.all_gather(w_qkv.astype(jnp.bfloat16), "own", axis=0, tiled=True),
        lax.all_gather(w_proj.astype(jnp.bfloat16), "own", axis=0, tiled=True),
        lax.all_gather(w_fc1.astype(jnp.bfloat16), "own", axis=0, tiled=True),
        lax.all_gather(w_fc2.astype(jnp.bfloat16), "own", axis=1, tiled=True),
        lax.all_gather(w_ada.astype(jnp.bfloat16), "own", axis=0, tiled=True),
        lax.all_gather(biases.astype(jnp.bfloat16), "own", axis=0, tiled=True),
    )
    full = (
        lax.all_gather(own_part[0], "dp", axis=1, tiled=True),
        lax.all_gather(own_part[1], "dp", axis=1, tiled=True),
        lax.all_gather(own_part[2], "dp", axis=1, tiled=True),
        lax.all_gather(own_part[3], "dp", axis=0, tiled=True),
        lax.all_gather(own_part[4], "dp", axis=1, tiled=True),
        lax.all_gather(own_part[5], "dp", axis=0, tiled=True),
    )
    block_out, grad_in, grad_cond, partials, bias_terms, cond_act, dmod_low = block_pass(
        tokens_in, condition, cotangent, full[0], full[1], full[2], full[3], full[4], full[5]
    )
    summed = (
        lax.psum_scatter(partials[0], "dp", scatter_dimension=1, tiled=True),
        lax.psum_scatter(partials[1], "dp", scatter_dimension=1, tiled=True),
        lax.psum_scatter(partials[2], "dp", scatter_dimension=1, tiled=True),
        lax.psum_scatter(partials[3], "dp", scatter_dimension=0, tiled=True),
        lax.psum_scatter(partials[4], "dp", scatter_dimension=1, tiled=True),
        lax.psum_scatter(bias_terms, "dp", scatter_dimension=0, tiled=True),
    )
    owned = (
        lax.psum_scatter(summed[0], "own", scatter_dimension=0, tiled=True),
        lax.psum_scatter(summed[1], "own", scatter_dimension=0, tiled=True),
        lax.psum_scatter(summed[2], "own", scatter_dimension=0, tiled=True),
        lax.psum_scatter(summed[3], "own", scatter_dimension=1, tiled=True),
        lax.psum_scatter(summed[4], "own", scatter_dimension=0, tiled=True),
        lax.psum_scatter(summed[5], "own", scatter_dimension=0, tiled=True),
    )
    tiles = (owned[0], owned[1], owned[2], owned[3], owned[4])
    bias_tile = owned[5]
    weights = (w_qkv, w_proj, w_fc1, w_fc2, w_ada)
    moments = (mom_qkv, mom_proj, mom_fc1, mom_fc2, mom_ada)
    fresh = [momentum_rate * moments[index] + tiles[index] for index in range(5)]
    oriented = [fresh[0], fresh[1], fresh[2], fresh[3].T, fresh[4]]
    squares = lax.psum(
        (
            jnp.sum(oriented[0] * oriented[0]),
            jnp.sum(oriented[1] * oriented[1]),
            jnp.sum(oriented[2] * oriented[2]),
            jnp.sum(oriented[3] * oriented[3]),
            jnp.sum(oriented[4] * oriented[4]),
        ),
        ("dp", "own"),
    )
    magnitudes = [jnp.sqrt(squares[index]) for index in range(5)]
    moment_norms = jnp.stack(magnitudes)
    iterate = [oriented[index] / (magnitudes[index] + 1e-07) for index in range(5)]
    highest = lax.Precision.HIGHEST
    for ns_step in range(NS_ITERS):
        columns = (
            lax.all_gather(for_sending(iterate[0]), "own", axis=0, tiled=True),
            lax.all_gather(for_sending(iterate[1]), "own", axis=0, tiled=True),
            lax.all_gather(for_sending(iterate[2]), "own", axis=0, tiled=True),
            lax.all_gather(for_sending(iterate[3]), "own", axis=0, tiled=True),
            lax.all_gather(for_sending(iterate[4]), "own", axis=0, tiled=True),
        )
        products = [
            jnp.dot(iterate[index], columns[index].T, precision=highest) for index in range(5)
        ]
        grams = (
            lax.psum(products[0].astype(jnp.bfloat16), "dp").astype(jnp.float32),
            lax.psum(products[1].astype(jnp.bfloat16), "dp").astype(jnp.float32),
            lax.psum(products[2].astype(jnp.bfloat16), "dp").astype(jnp.float32),
            lax.psum(products[3].astype(jnp.bfloat16), "dp").astype(jnp.float32),
            lax.psum(products[4].astype(jnp.bfloat16), "dp").astype(jnp.float32),
        )
        gram_full = (
            lax.all_gather(grams[0].astype(jnp.bfloat16), "own", axis=0, tiled=True).astype(
                jnp.float32
            ),
            lax.all_gather(grams[1].astype(jnp.bfloat16), "own", axis=0, tiled=True).astype(
                jnp.float32
            ),
            lax.all_gather(grams[2].astype(jnp.bfloat16), "own", axis=0, tiled=True).astype(
                jnp.float32
            ),
            lax.all_gather(grams[3].astype(jnp.bfloat16), "own", axis=0, tiled=True).astype(
                jnp.float32
            ),
            lax.all_gather(grams[4].astype(jnp.bfloat16), "own", axis=0, tiled=True).astype(
                jnp.float32
            ),
        )
        next_iterate = []
        for index in range(5):
            square = jnp.dot(grams[index], gram_full[index], precision=highest)
            mixer = coef_second * grams[index] + coef_third * square
            updated = coef_first * iterate[index] + jnp.dot(
                mixer, columns[index], precision=highest
            )
            next_iterate.append(updated)
        iterate = next_iterate
    ortho = [iterate[0], iterate[1], iterate[2], iterate[3].T, iterate[4]]
    updated_weights = []
    for index in range(5):
        whole_shape = full[index].shape
        factor = 0.2 * math.sqrt(max(whole_shape[0], whole_shape[1]))
        updated_weights.append(weights[index] - learn_rate * factor * ortho[index])
    moment_bias = momentum_rate * bias_mom + bias_tile
    new_bias = biases - bias_rate * moment_bias
    return (
        block_out,
        grad_in,
        grad_cond,
        tiles[0],
        tiles[1],
        tiles[2],
        tiles[3],
        tiles[4],
        bias_tile,
        updated_weights[0],
        updated_weights[1],
        updated_weights[2],
        updated_weights[3],
        updated_weights[4],
        fresh[0],
        fresh[1],
        fresh[2],
        fresh[3],
        fresh[4],
        new_bias,
        moment_bias,
        moment_norms,
    )


def solution(mesh):
    placed = (
        P(("dp", "own"), None, None),
        P(("dp", "own"), None),
        P(("dp", "own"), None, None),
        P("own", "dp"),
        P("own", "dp"),
        P("own", "dp"),
        P("dp", "own"),
        P("own", "dp"),
        P("own", "dp"),
        P("own", "dp"),
        P("own", "dp"),
        P("dp", "own"),
        P("own", "dp"),
        P(("dp", "own")),
        P(("dp", "own")),
    )
    return jax.shard_map(
        per_device,
        mesh=mesh,
        in_specs=placed,
        out_specs=(
            P(("dp", "own"), None, None),
            P(("dp", "own"), None, None),
            P(("dp", "own"), None),
            P("own", "dp"),
            P("own", "dp"),
            P("own", "dp"),
            P("dp", "own"),
            P("own", "dp"),
            P(("dp", "own")),
            P("own", "dp"),
            P("own", "dp"),
            P("own", "dp"),
            P("dp", "own"),
            P("own", "dp"),
            P("own", "dp"),
            P("own", "dp"),
            P("own", "dp"),
            P("dp", "own"),
            P("own", "dp"),
            P(("dp", "own")),
            P(("dp", "own")),
            P(),
        ),
        check_vma=False,
    )
```

profile of v0, /device:TPU:0, one launch (start us, length us, event | category | flops | bytes accessed | tf_op | source)
XLA Modules:
  0.0 2185.7 jit_solution(3009070349646886199)
XLA Ops:
  78.5 27.1 %all-reduce.1 = bf16[10752]{0:T(1024)(128)(2,1)S(1)} all-reduce(bf16[10752]{0:T(1024)(128)(2,1)S(1)} %dynamic-update-slice.1), channel_id=1, replica_groups=mesh['dp'=8,'own'=4] {'dp'}, use_global_device_ids=true, to_apply=%add.1 | all-reduce | flops 10752 | bytes 43008
  111.3 27.0 %all-gather.33.cloned.1.call-done = bf16[768,2304]{0,1:T(8,128)(2,1)} async-done(((bf16[768,288]{0,1:T(8,128)(2,1)}), bf16[768,2304]{0,1:T(8,128)(2,1)}) %all-gather.33.cloned.1.call-update) | async-done | bytes 3538960 | tf_op jit(solution)/shard_map/all_gather | solution.py:204
  167.1 47.7 %all-gather.37.cloned.1.call-done = bf16[768,3072]{1,0:T(8,128)(2,1)} async-done(((bf16[768,384]{1,0:T(8,128)(2,1)}), bf16[768,3072]{1,0:T(8,128)(2,1)}) %all-gather.37.cloned.1.call-update) | async-done | bytes 4718608 | tf_op jit(solution)/shard_map/all_gather | solution.py:206
  221.7 44.7 %all-gather.39.cloned.1.call-done = bf16[3072,768]{0,1:T(8,128)(2,1)} async-done(((bf16[384,768]{0,1:T(8,128)(2,1)}), bf16[3072,768]{0,1:T(8,128)(2,1)}) %all-gather.39.cloned.1.call-update) | async-done | bytes 4718608 | tf_op jit(solution)/shard_map/all_gather | solution.py:207
  376.8 39.7 %reduce-scatter.17.cloned.1.call-done = f32[768,288]{0,1:T(8,128)} async-done(((f32[768,2304]{0,1:T(8,128)}), f32[768,288]{0,1:T(8,128)}) %reduce-scatter.17.cloned.1.call-update) | async-done | bytes 884752 | tf_op jit(solution)/shard_map/reduce_scatter | solution.py:215
  419.2 97.6 %reduce-scatter.21.cloned.1.call-done = f32[768,384]{1,0:T(8,128)} async-done(((f32[768,3072]{1,0:T(8,128)}), f32[768,384]{1,0:T(8,128)}) %reduce-scatter.21.cloned.1.call-update) | async-done | bytes 1179664 | tf_op jit(solution)/shard_map/reduce_scatter | solution.py:217
  516.9 100.2 %reduce-scatter.25.cloned.1.call-done = f32[384,768]{0,1:T(8,128)} async-done(((f32[3072,768]{0,1:T(8,128)}), f32[384,768]{0,1:T(8,128)}) %reduce-scatter.25.cloned.1.call-update) | async-done | bytes 1179664 | tf_op jit(solution)/shard_map/reduce_scatter | solution.py:218
  617.1 144.6 %reduce-scatter.29.cloned.1.call-done = f32[768,576]{0,1:T(8,128)} async-done(((f32[768,4608]{0,1:T(8,128)}), f32[768,576]{0,1:T(8,128)}) %reduce-scatter.29.cloned.1.call-update) | async-done | bytes 1769488 | tf_op jit(solution)/shard_map/reduce_scatter | solution.py:219
  790.3 30.6 %reduce-scatter.31.cloned.1.call-done = f32[192,288]{1,0:T(8,128)} async-done(((f32[768,288]{1,0:T(8,128)}), f32[192,288]{1,0:T(8,128)}) %reduce-scatter.31.cloned.1.call-update) | async-done | bytes 221200
  822.6 30.6 %reduce-scatter.23.cloned.1.call-done = f32[192,384]{1,0:T(8,128)} async-done(((f32[768,384]{1,0:T(8,128)}), f32[192,384]{1,0:T(8,128)}) %reduce-scatter.23.cloned.1.call-update) | async-done | bytes 294928 | tf_op jit(solution)/shard_map/reduce_scatter | solution.py:225
  854.8 30.5 %reduce-scatter.27.cloned.1.call-done = f32[384,192]{0,1:T(8,128)} async-done(((f32[384,768]{0,1:T(8,128)}), f32[384,192]{0,1:T(8,128)}) %reduce-scatter.27.cloned.1.call-update) | async-done | bytes 294928 | tf_op jit(solution)/shard_map/reduce_scatter | solution.py:226
  886.9 36.0 %reduce-scatter.35.cloned.1.call-done = f32[192,576]{1,0:T(8,128)} async-done(((f32[768,576]{1,0:T(8,128)}), f32[192,576]{1,0:T(8,128)}) %reduce-scatter.35.cloned.1.call-update) | async-done | bytes 442384
  924.7 39.7 %all-reduce.4 = (f32[]{:T(128)}, f32[]{:T(128)}, f32[]{:T(128)}, f32[]{:T(128)}, f32[]{:T(128)}) all-reduce(f32[]{:T(128)} %get-tuple-element.188, f32[]{:T(128)} %get-tuple-element.186, f32[]{:T(128)} %get-tuple-element.184, f32[]{:T(128)} %get-tuple-element.182, f32[]{:T(128)} %get-tuple-element.180), channel_id=1, replica_groups=mesh['dp'=8,'own'=4] {'dp','own'}, use_global_device_ids=true, to_apply=%region_36.37 | all-reduce | flops 5 | bytes 40 | tf_op jit(solution)/shard_map/psum | solution.py:236
  1028.5 60.7 %all-reduce.24.cloned.1.call-done = (bf16[192,768]{1,0:T(8,128)(2,1)}, bf16[192,768]{1,0:T(8,128)(2,1)}, bf16[192,768]{1,0:T(8,128)(2,1)}, bf16[192,768]{1,0:T(8,128)(2,1)}, bf16[192,768]{1,0:T(8,128)(2,1)}) async-done(((bf16[192,768]{1,0:T(8,128)(2,1)}, bf16[192,768]{1,0:T(8,128)(2,1)}, bf16[192,768]{1,0:T(8,128)(2,1)}, bf16[192,768]{1,0:T(8,128)(2,1)}, bf16[192,768]{1,0:T(8,128)(2,1)}), ...) | async-done | bytes 1474576 | tf_op jit(solution)/shard_map/psum | solution.py:262
  1092.0 26.2 %all-gather.51.cloned.1.call-done = bf16[768,768]{1,0:T(8,128)(2,1)} async-done(((bf16[192,768]{1,0:T(8,128)(2,1)}), bf16[768,768]{1,0:T(8,128)(2,1)}) %all-gather.51.cloned.1.call-update) | async-done | bytes 1179664 | tf_op jit(solution)/shard_map/all_gather | solution.py:272
  1262.4 61.8 %all-reduce.22.cloned.1.call-done = (bf16[192,768]{1,0:T(8,128)(2,1)}, bf16[192,768]{1,0:T(8,128)(2,1)}, bf16[192,768]{1,0:T(8,128)(2,1)}, bf16[192,768]{1,0:T(8,128)(2,1)}, bf16[192,768]{1,0:T(8,128)(2,1)}) async-done(((bf16[192,768]{1,0:T(8,128)(2,1)}, bf16[192,768]{1,0:T(8,128)(2,1)}, bf16[192,768]{1,0:T(8,128)(2,1)}, bf16[192,768]{1,0:T(8,128)(2,1)}, bf16[192,768]{1,0:T(8,128)(2,1)}), ...) | async-done | bytes 1474576 | tf_op jit(solution)/shard_map/psum | solution.py:262
  1326.7 26.5 %all-gather.53.cloned.1.call-done = bf16[768,768]{1,0:T(8,128)(2,1)} async-done(((bf16[192,768]{1,0:T(8,128)(2,1)}), bf16[768,768]{1,0:T(8,128)(2,1)}) %all-gather.53.cloned.1.call-update) | async-done | bytes 1179664 | tf_op jit(solution)/shard_map/all_gather | solution.py:272
  1496.4 61.6 %all-reduce.20.cloned.1.call-done = (bf16[192,768]{1,0:T(8,128)(2,1)}, bf16[192,768]{1,0:T(8,128)(2,1)}, bf16[192,768]{1,0:T(8,128)(2,1)}, bf16[192,768]{1,0:T(8,128)(2,1)}, bf16[192,768]{1,0:T(8,128)(2,1)}) async-done(((bf16[192,768]{1,0:T(8,128)(2,1)}, bf16[192,768]{1,0:T(8,128)(2,1)}, bf16[192,768]{1,0:T(8,128)(2,1)}, bf16[192,768]{1,0:T(8,128)(2,1)}, bf16[192,768]{1,0:T(8,128)(2,1)}), ...) | async-done | bytes 1474576 | tf_op jit(solution)/shard_map/psum | solution.py:262
  1560.7 26.3 %all-gather.55.cloned.1.call-done = bf16[768,768]{1,0:T(8,128)(2,1)} async-done(((bf16[192,768]{1,0:T(8,128)(2,1)}), bf16[768,768]{1,0:T(8,128)(2,1)}) %all-gather.55.cloned.1.call-update) | async-done | bytes 1179664 | tf_op jit(solution)/shard_map/all_gather | solution.py:272
  1731.5 61.7 %all-reduce.18.cloned.1.call-done = (bf16[192,768]{1,0:T(8,128)(2,1)}, bf16[192,768]{1,0:T(8,128)(2,1)}, bf16[192,768]{1,0:T(8,128)(2,1)}, bf16[192,768]{1,0:T(8,128)(2,1)}, bf16[192,768]{1,0:T(8,128)(2,1)}) async-done(((bf16[192,768]{1,0:T(8,128)(2,1)}, bf16[192,768]{1,0:T(8,128)(2,1)}, bf16[192,768]{1,0:T(8,128)(2,1)}, bf16[192,768]{1,0:T(8,128)(2,1)}, bf16[192,768]{1,0:T(8,128)(2,1)}), ...) | async-done | bytes 1474576 | tf_op jit(solution)/shard_map/psum | solution.py:262
  1795.8 26.5 %all-gather.57.cloned.1.call-done = bf16[768,768]{1,0:T(8,128)(2,1)} async-done(((bf16[192,768]{1,0:T(8,128)(2,1)}), bf16[768,768]{1,0:T(8,128)(2,1)}) %all-gather.57.cloned.1.call-update) | async-done | bytes 1179664 | tf_op jit(solution)/shard_map/all_gather | solution.py:272
  1967.3 61.7 %all-reduce.16.cloned.1.call-done = (bf16[192,768]{1,0:T(8,128)(2,1)}, bf16[192,768]{1,0:T(8,128)(2,1)}, bf16[192,768]{1,0:T(8,128)(2,1)}, bf16[192,768]{1,0:T(8,128)(2,1)}, bf16[192,768]{1,0:T(8,128)(2,1)}) async-done(((bf16[192,768]{1,0:T(8,128)(2,1)}, bf16[192,768]{1,0:T(8,128)(2,1)}, bf16[192,768]{1,0:T(8,128)(2,1)}, bf16[192,768]{1,0:T(8,128)(2,1)}, bf16[192,768]{1,0:T(8,128)(2,1)}), ...) | async-done | bytes 1474576 | tf_op jit(solution)/shard_map/psum | solution.py:262
  2045.8 27.6 %all-reduce.2 = f32[10752]{0:T(1024)} all-reduce(f32[10752]{0:T(1024)} %constant_dynamic-update-slice_fusion.10), channel_id=12, replica_groups=mesh['dp'=8,'own'=4] {'dp'}, use_global_device_ids=true, to_apply=%region_33.34.clone | all-reduce | flops 10752 | bytes 86016
  2120.1 26.2 %all-gather.89.cloned.1.call-done = bf16[768,768]{1,0:T(8,128)(2,1)} async-done(((bf16[192,768]{1,0:T(8,128)(2,1)}), bf16[768,768]{1,0:T(8,128)(2,1)}) %all-gather.89.cloned.1.call-update) | async-done | bytes 1179664 | tf_op jit(solution)/shard_map/all_gather | solution.py:281
  (587 shorter events, 1000.3 us)
Async XLA Ops:
  36.4 125.9 %all-gather.35.cloned.1.call-start = ((), (), s32[]{:S(2)}) async-start(), calls=%async_computation.12 | async-start | bytes 1327104 | tf_op jit(solution)/shard_map/all_gather | solution.py:205
  44.6 170.2 %all-gather.37.cloned.1.call-start = ((), (), s32[]{:S(2)}) async-start(), calls=%async_computation.13 | async-start | bytes 5308416 | tf_op jit(solution)/shard_map/all_gather | solution.py:206
  56.4 210.0 %all-gather.39.cloned.1.call-start = ((), (), s32[]{:S(2)}) async-start(), calls=%async_computation.14 | async-start | bytes 5308416 | tf_op jit(solution)/shard_map/all_gather | solution.py:207
  67.1 307.8 %reduce-scatter.19.cloned.1.call-start = ((), (), s32[]{:S(2)}) async-start(), calls=%async_computation.16 | async-start | bytes 2654208 | tf_op jit(solution)/shard_map/reduce_scatter | solution.py:216
  294.5 122.1 %reduce-scatter.17.cloned.1.call-start = ((), (), s32[]{:S(2)}) async-start(), calls=%async_computation.15 | async-start | bytes 7962624 | tf_op jit(solution)/shard_map/reduce_scatter | solution.py:215
  340.5 176.3 %reduce-scatter.21.cloned.1.call-start = ((), (), s32[]{:S(2)}) async-start(), calls=%async_computation.17 | async-start | bytes 10616832 | tf_op jit(solution)/shard_map/reduce_scatter | solution.py:217
  348.7 268.4 %reduce-scatter.25.cloned.1.call-start = ((), (), s32[]{:S(2)}) async-start(), calls=%async_computation.19 | async-start | bytes 10616832 | tf_op jit(solution)/shard_map/reduce_scatter | solution.py:218
  359.2 402.4 %reduce-scatter.29.cloned.1.call-start = ((), (), s32[]{:S(2)}) async-start(), calls=%async_computation.21 | async-start | bytes 15925248 | tf_op jit(solution)/shard_map/reduce_scatter | solution.py:219
  374.8 414.0 %reduce-scatter.33.cloned.1.call-start = ((), (), s32[]{:S(2)}) async-start(), calls=%async_computation.48 | async-start | bytes 491520
  376.8 444.2 %reduce-scatter.31.cloned.1.call-start = ((), (), s32[]{:S(2)}) async-start(), calls=%async_computation.47 | async-start | bytes 1474560
  419.1 434.0 %reduce-scatter.23.cloned.1.call-start = ((), (), s32[]{:S(2)}) async-start(), calls=%async_computation.18 | async-start | bytes 1474560 | tf_op jit(solution)/shard_map/reduce_scatter | solution.py:225
  516.8 368.5 %reduce-scatter.27.cloned.1.call-start = ((), (), s32[]{:S(2)}) async-start(), calls=%async_computation.20 | async-start | bytes 1474560 | tf_op jit(solution)/shard_map/reduce_scatter | solution.py:226
  617.1 305.9 %reduce-scatter.35.cloned.1.call-start = ((), (), s32[]{:S(2)}) async-start(), calls=%async_computation.49 | async-start | bytes 2457600
  764.5 324.7 %all-reduce.24.cloned.1.call-start = ((), (), s32[]{:S(2)}) async-start(), calls=%async_computation.54 | async-start | bytes 2949120 | tf_op jit(solution)/shard_map/psum | solution.py:262
  1091.2 150.6 %all-gather.41.cloned.1.call-start = ((), (), s32[]{:S(2)}) async-start(), calls=%async_computation.22 | async-start | bytes 1474560 | tf_op jit(solution)/shard_map/all_gather | solution.py:269
  1091.9 232.2 %all-reduce.22.cloned.1.call-start = ((), (), s32[]{:S(2)}) async-start(), calls=%async_computation.53 | async-start | bytes 2949120 | tf_op jit(solution)/shard_map/psum | solution.py:262
  1326.1 150.0 %all-gather.43.cloned.1.call-start = ((), (), s32[]{:S(2)}) async-start(), calls=%async_computation.23 | async-start | bytes 1474560 | tf_op jit(solution)/shard_map/all_gather | solution.py:269
  1326.7 231.3 %all-reduce.20.cloned.1.call-start = ((), (), s32[]{:S(2)}) async-start(), calls=%async_computation.52 | async-start | bytes 2949120 | tf_op jit(solution)/shard_map/psum | solution.py:262
  1560.1 150.8 %all-gather.45.cloned.1.call-start = ((), (), s32[]{:S(2)}) async-start(), calls=%async_computation.24 | async-start | bytes 1474560 | tf_op jit(solution)/shard_map/all_gather | solution.py:269
  1560.7 232.6 %all-reduce.18.cloned.1.call-start = ((), (), s32[]{:S(2)}) async-start(), calls=%async_computation.51 | async-start | bytes 2949120 | tf_op jit(solution)/shard_map/psum | solution.py:262
  1795.2 150.6 %all-gather.47.cloned.1.call-start = ((), (), s32[]{:S(2)}) async-start(), calls=%async_computation.25 | async-start | bytes 1474560 | tf_op jit(solution)/shard_map/all_gather | solution.py:269
  1795.7 233.3 %all-reduce.16.cloned.1.call-start = ((), (), s32[]{:S(2)}) async-start(), calls=%async_computation.50 | async-start | bytes 2949120 | tf_op jit(solution)/shard_map/psum | solution.py:262
  1967.3 129.2 %all-gather.59.cloned.1.call-start = ((), (), s32[]{:S(2)}) async-start(), calls=%async_computation.31 | async-start | bytes 1474560 | tf_op jit(solution)/shard_map/all_gather | solution.py:272
  2043.1 132.5 %all-gather.79.cloned.1.call-start = ((), (), s32[]{:S(2)}) async-start(), calls=%async_computation.41 | async-start | bytes 1474560 | tf_op jit(solution)/shard_map/all_gather | solution.py:278
  (151 other events, 6300.6 us)
Sparse Core Ops, SparseCore 0:
  24.2 71.8 all-gather.30
  98.2 40.0 all-gather.32
  163.7 51.0 all-gather.36
  216.3 50.0 all-gather.38
  294.6 35.5 reduce-scatter.18
  340.7 75.8 reduce-scatter.16
  418.9 97.8 reduce-scatter.20
  519.1 97.8 reduce-scatter.24
  619.2 142.4 reduce-scatter.28
  888.8 34.1 reduce-scatter.34
  1028.6 60.6 all-reduce.23
  1180.2 29.1 all-gather.80
  1211.2 30.5 all-gather.40
  1262.5 61.6 all-reduce.21
  1414.5 29.1 all-gather.82
  1445.4 30.5 all-gather.42
  1496.5 61.4 all-reduce.19
  1618.4 29.1 all-gather.64
  1649.4 29.0 all-gather.84
  1680.2 30.6 all-gather.44
  1731.5 61.6 all-reduce.17
  1853.3 29.1 all-gather.66
  1915.0 30.6 all-gather.46
  1967.4 61.6 all-reduce.15
  (21 shorter events, 573.1 us)
where the time goes:
time: 2190 us
  waiting for transfers between devices  1390 us (63%)
  blocking collectives  472 us (22%)
  matrix products  231 us (11%)
  local copies, waits for them, and re-layouts  43.6 us (2%)
  other arithmetic  26.6 us (1%)
  between operations  22.4 us (1%)
    psum x5, waiting for transfers between devices, per_device(): lax.psum(products[0].astype(jnp.bfloat16), 'dp').astype(jnp.float32)  308 us
    reduce_scatter x1, waiting for transfers between devices, per_device(): lax.psum_scatter(partials[4], 'dp', scatter_dimension=1, tiled=True)  145 us
    all_gather x5, waiting for transfers between devices, per_device(): lax.all_gather(grams[1].astype(jnp.bfloat16), 'own', axis=0, tiled=True)  105 us
    unnamed x48, waiting for transfers between devices  102 us
    reduce_scatter x1, waiting for transfers between devices, per_device(): lax.psum_scatter(partials[3], 'dp', scatter_dimension=0, tiled=True)  100 us
    reduce_scatter x1, waiting for transfers between devices, per_device(): lax.psum_scatter(partials[2], 'dp', scatter_dimension=1, tiled=True)  97.6 us
    all_gather x5, waiting for transfers between devices, per_device(): lax.all_gather(grams[3].astype(jnp.bfloat16), 'own', axis=0, tiled=True)  93.2 us
    all_gather x5, waiting for transfers between devices, per_device(): lax.all_gather(grams[4].astype(jnp.bfloat16), 'own', axis=0, tiled=True)  83.7 us
  transfers between devices with their start and end apart: 45, of which 41 were waited for; matrix products, arithmetic and copies ran while one was open for 9% of the time, Pallas kernels for 0%

commit v1 on v0

--- a/solution.py
+++ b/solution.py
@@ -259,7 +259,9 @@
             jnp.dot(iterate[index], columns[index].T, precision=highest) for index in range(5)
         ]
         grams = (
-            lax.psum(products[0].astype(jnp.bfloat16), "dp").astype(jnp.float32),
+            jnp.sum(lax.all_gather(products[0].astype(jnp.bfloat16), "dp"), axis=0).astype(
+                jnp.float32
+            ),
             lax.psum(products[1].astype(jnp.bfloat16), "dp").astype(jnp.float32),
             lax.psum(products[2].astype(jnp.bfloat16), "dp").astype(jnp.float32),
             lax.psum(products[3].astype(jnp.bfloat16), "dp").astype(jnp.float32),

time: 2190 us -> 2260 us (1.032)
  waiting for transfers between devices: 1390 us -> 1440 us
    all_gather x5, waiting for transfers between devices: 65.5 us -> 133 us  [per_device(): lax.all_gather(grams[0].astype(jnp.bfloat16), 'own', axis=0, tiled=True)]
    all_gather x5, waiting for transfers between devices: 105 us -> 52 us  [per_device(): lax.all_gather(grams[1].astype(jnp.bfloat16), 'own', axis=0, tiled=True)]
    all_gather x0 -> x5, waiting for transfers between devices: none -> 49.5 us  [per_device(): lax.all_gather(products[0].astype(jnp.bfloat16), 'dp')]
    unnamed x48 -> x53, waiting for transfers between devices: 102 us -> 99.8 us
  transfers between devices with their start and end apart: 45 -> 50, of which waited for: 41 -> 46; matrix products, arithmetic and copies ran while one was open for 9% -> 11% of each run, Pallas kernels for 0% -> 0%
where the time goes in v1:
time: 2260 us; the launch traced here: 2250 us
  waiting for transfers between devices  1440 us (64%)
  blocking collectives  469 us (21%)
  matrix products  227 us (10%)
  local copies, waits for them, and re-layouts  46.1 us (2%)
  other arithmetic  40.5 us (2%)
  between operations  22.6 us (1%)
    psum x5, waiting for transfers between devices, per_device(): lax.psum(products[1].astype(jnp.bfloat16), 'dp').astype(jnp.float32)  298 us
    reduce_scatter x1, waiting for transfers between devices, per_device(): lax.psum_scatter(partials[4], 'dp', scatter_dimension=1, tiled=True)  145 us
    all_gather x5, waiting for transfers between devices, per_device(): lax.all_gather(grams[0].astype(jnp.bfloat16), 'own', axis=0, tiled=True)  133 us
    reduce_scatter x1, waiting for transfers between devices, per_device(): lax.psum_scatter(partials[3], 'dp', scatter_dimension=0, tiled=True)  100 us
    unnamed x53, waiting for transfers between devices  99.8 us
    reduce_scatter x1, waiting for transfers between devices, per_device(): lax.psum_scatter(partials[2], 'dp', scatter_dimension=1, tiled=True)  97.6 us
    all_gather x5, waiting for transfers between devices, per_device(): lax.all_gather(grams[3].astype(jnp.bfloat16), 'own', axis=0, tiled=True)  94.2 us
    all_gather x5, waiting for transfers between devices, per_device(): lax.all_gather(grams[4].astype(jnp.bfloat16), 'own', axis=0, tiled=True)  84.7 us
  transfers between devices with their start and end apart: 50, of which 46 were waited for; matrix products, arithmetic and copies ran while one was open for 11% of the time, Pallas kernels for 0%

profile of v1, /device:TPU:0, one launch (start us, length us, event | category | flops | bytes accessed | tf_op | source)
XLA Modules:
  0.0 2252.7 jit_solution(15174826304017888269)
XLA Ops:
  78.5 27.1 %all-reduce.1 = bf16[10752]{0:T(1024)(128)(2,1)S(1)} all-reduce(bf16[10752]{0:T(1024)(128)(2,1)S(1)} %dynamic-update-slice.1), channel_id=1, replica_groups=mesh['dp'=8,'own'=4] {'dp'}, use_global_device_ids=true, to_apply=%add.1 | all-reduce | flops 10752 | bytes 43008
  111.3 27.0 %all-gather.43.cloned.1.call-done = bf16[768,2304]{0,1:T(8,128)(2,1)} async-done(((bf16[768,288]{0,1:T(8,128)(2,1)}), bf16[768,2304]{0,1:T(8,128)(2,1)}) %all-gather.43.cloned.1.call-update) | async-done | bytes 3538960 | tf_op jit(solution)/shard_map/all_gather | solution.py:204
  167.1 47.7 %all-gather.47.cloned.1.call-done = bf16[768,3072]{1,0:T(8,128)(2,1)} async-done(((bf16[768,384]{1,0:T(8,128)(2,1)}), bf16[768,3072]{1,0:T(8,128)(2,1)}) %all-gather.47.cloned.1.call-update) | async-done | bytes 4718608 | tf_op jit(solution)/shard_map/all_gather | solution.py:206
  221.7 44.7 %all-gather.49.cloned.1.call-done = bf16[3072,768]{0,1:T(8,128)(2,1)} async-done(((bf16[384,768]{0,1:T(8,128)(2,1)}), bf16[3072,768]{0,1:T(8,128)(2,1)}) %all-gather.49.cloned.1.call-update) | async-done | bytes 4718608 | tf_op jit(solution)/shard_map/all_gather | solution.py:207
  376.7 39.8 %reduce-scatter.17.cloned.1.call-done = f32[768,288]{0,1:T(8,128)} async-done(((f32[768,2304]{0,1:T(8,128)}), f32[768,288]{0,1:T(8,128)}) %reduce-scatter.17.cloned.1.call-update) | async-done | bytes 884752 | tf_op jit(solution)/shard_map/reduce_scatter | solution.py:215
  419.2 97.6 %reduce-scatter.21.cloned.1.call-done = f32[768,384]{1,0:T(8,128)} async-done(((f32[768,3072]{1,0:T(8,128)}), f32[768,384]{1,0:T(8,128)}) %reduce-scatter.21.cloned.1.call-update) | async-done | bytes 1179664 | tf_op jit(solution)/shard_map/reduce_scatter | solution.py:217
  516.8 100.2 %reduce-scatter.25.cloned.1.call-done = f32[384,768]{0,1:T(8,128)} async-done(((f32[3072,768]{0,1:T(8,128)}), f32[384,768]{0,1:T(8,128)}) %reduce-scatter.25.cloned.1.call-update) | async-done | bytes 1179664 | tf_op jit(solution)/shard_map/reduce_scatter | solution.py:218
  617.1 144.6 %reduce-scatter.29.cloned.1.call-done = f32[768,576]{0,1:T(8,128)} async-done(((f32[768,4608]{0,1:T(8,128)}), f32[768,576]{0,1:T(8,128)}) %reduce-scatter.29.cloned.1.call-update) | async-done | bytes 1769488 | tf_op jit(solution)/shard_map/reduce_scatter | solution.py:219
  790.3 30.6 %reduce-scatter.31.cloned.1.call-done = f32[192,288]{1,0:T(8,128)} async-done(((f32[768,288]{1,0:T(8,128)}), f32[192,288]{1,0:T(8,128)}) %reduce-scatter.31.cloned.1.call-update) | async-done | bytes 221200
  822.5 30.6 %reduce-scatter.23.cloned.1.call-done = f32[192,384]{1,0:T(8,128)} async-done(((f32[768,384]{1,0:T(8,128)}), f32[192,384]{1,0:T(8,128)}) %reduce-scatter.23.cloned.1.call-update) | async-done | bytes 294928 | tf_op jit(solution)/shard_map/reduce_scatter | solution.py:225
  854.8 30.5 %reduce-scatter.27.cloned.1.call-done = f32[384,192]{0,1:T(8,128)} async-done(((f32[384,768]{0,1:T(8,128)}), f32[384,192]{0,1:T(8,128)}) %reduce-scatter.27.cloned.1.call-update) | async-done | bytes 294928 | tf_op jit(solution)/shard_map/reduce_scatter | solution.py:226
  886.9 36.0 %reduce-scatter.35.cloned.1.call-done = f32[192,576]{1,0:T(8,128)} async-done(((f32[768,576]{1,0:T(8,128)}), f32[192,576]{1,0:T(8,128)}) %reduce-scatter.35.cloned.1.call-update) | async-done | bytes 442384
  924.7 39.7 %all-reduce.4 = (f32[]{:T(128)}, f32[]{:T(128)}, f32[]{:T(128)}, f32[]{:T(128)}, f32[]{:T(128)}) all-reduce(f32[]{:T(128)} %get-tuple-element.183, f32[]{:T(128)} %get-tuple-element.181, f32[]{:T(128)} %get-tuple-element.179, f32[]{:T(128)} %get-tuple-element.177, f32[]{:T(128)} %get-tuple-element.175), channel_id=1, replica_groups=mesh['dp'=8,'own'=4] {'dp','own'}, use_global_device_ids=true, to_apply=%region_36.37 | all-reduce | flops 5 | bytes 40 | tf_op jit(solution)/shard_map/psum | solution.py:236
  1016.8 59.6 %all-reduce.24.cloned.1.call-done = (bf16[192,768]{1,0:T(8,128)(2,1)}, bf16[192,768]{1,0:T(8,128)(2,1)}, bf16[192,768]{1,0:T(8,128)(2,1)}, bf16[192,768]{1,0:T(8,128)(2,1)}) async-done(((bf16[192,768]{1,0:T(8,128)(2,1)}, bf16[192,768]{1,0:T(8,128)(2,1)}, bf16[192,768]{1,0:T(8,128)(2,1)}, bf16[192,768]{1,0:T(8,128)(2,1)}), (bf16[192,768]{1,0:T(8,128)(2,1)}, bf16[192,768]{1,0:T(8,128)(2,1)}, ...) | async-done | bytes 1179664 | tf_op jit(solution)/shard_map/psum | solution.py:265
  1232.7 59.7 %all-reduce.22.cloned.1.call-done = (bf16[192,768]{1,0:T(8,128)(2,1)}, bf16[192,768]{1,0:T(8,128)(2,1)}, bf16[192,768]{1,0:T(8,128)(2,1)}, bf16[192,768]{1,0:T(8,128)(2,1)}) async-done(((bf16[192,768]{1,0:T(8,128)(2,1)}, bf16[192,768]{1,0:T(8,128)(2,1)}, bf16[192,768]{1,0:T(8,128)(2,1)}, bf16[192,768]{1,0:T(8,128)(2,1)}), (bf16[192,768]{1,0:T(8,128)(2,1)}, bf16[192,768]{1,0:T(8,128)(2,1)}, ...) | async-done | bytes 1179664 | tf_op jit(solution)/shard_map/psum | solution.py:265
  1294.8 26.7 %all-gather.51.cloned.1.call-done = bf16[768,768]{1,0:T(8,128)(2,1)} async-done(((bf16[192,768]{1,0:T(8,128)(2,1)}), bf16[768,768]{1,0:T(8,128)(2,1)}) %all-gather.51.cloned.1.call-update) | async-done | bytes 1179664 | tf_op jit(solution)/shard_map/all_gather | solution.py:271
  1478.8 59.7 %all-reduce.20.cloned.1.call-done = (bf16[192,768]{1,0:T(8,128)(2,1)}, bf16[192,768]{1,0:T(8,128)(2,1)}, bf16[192,768]{1,0:T(8,128)(2,1)}, bf16[192,768]{1,0:T(8,128)(2,1)}) async-done(((bf16[192,768]{1,0:T(8,128)(2,1)}, bf16[192,768]{1,0:T(8,128)(2,1)}, bf16[192,768]{1,0:T(8,128)(2,1)}, bf16[192,768]{1,0:T(8,128)(2,1)}), (bf16[192,768]{1,0:T(8,128)(2,1)}, bf16[192,768]{1,0:T(8,128)(2,1)}, ...) | async-done | bytes 1179664 | tf_op jit(solution)/shard_map/psum | solution.py:265
  1540.7 26.8 %all-gather.53.cloned.1.call-done = bf16[768,768]{1,0:T(8,128)(2,1)} async-done(((bf16[192,768]{1,0:T(8,128)(2,1)}), bf16[768,768]{1,0:T(8,128)(2,1)}) %all-gather.53.cloned.1.call-update) | async-done | bytes 1179664 | tf_op jit(solution)/shard_map/all_gather | solution.py:271
  1725.6 59.5 %all-reduce.18.cloned.1.call-done = (bf16[192,768]{1,0:T(8,128)(2,1)}, bf16[192,768]{1,0:T(8,128)(2,1)}, bf16[192,768]{1,0:T(8,128)(2,1)}, bf16[192,768]{1,0:T(8,128)(2,1)}) async-done(((bf16[192,768]{1,0:T(8,128)(2,1)}, bf16[192,768]{1,0:T(8,128)(2,1)}, bf16[192,768]{1,0:T(8,128)(2,1)}, bf16[192,768]{1,0:T(8,128)(2,1)}), (bf16[192,768]{1,0:T(8,128)(2,1)}, bf16[192,768]{1,0:T(8,128)(2,1)}, ...) | async-done | bytes 1179664 | tf_op jit(solution)/shard_map/psum | solution.py:265
  1787.3 26.8 %all-gather.55.cloned.1.call-done = bf16[768,768]{1,0:T(8,128)(2,1)} async-done(((bf16[192,768]{1,0:T(8,128)(2,1)}), bf16[768,768]{1,0:T(8,128)(2,1)}) %all-gather.55.cloned.1.call-update) | async-done | bytes 1179664 | tf_op jit(solution)/shard_map/all_gather | solution.py:271
  1972.4 59.5 %all-reduce.16.cloned.1.call-done = (bf16[192,768]{1,0:T(8,128)(2,1)}, bf16[192,768]{1,0:T(8,128)(2,1)}, bf16[192,768]{1,0:T(8,128)(2,1)}, bf16[192,768]{1,0:T(8,128)(2,1)}) async-done(((bf16[192,768]{1,0:T(8,128)(2,1)}, bf16[192,768]{1,0:T(8,128)(2,1)}, bf16[192,768]{1,0:T(8,128)(2,1)}, bf16[192,768]{1,0:T(8,128)(2,1)}), (bf16[192,768]{1,0:T(8,128)(2,1)}, bf16[192,768]{1,0:T(8,128)(2,1)}, ...) | async-done | bytes 1179664 | tf_op jit(solution)/shard_map/psum | solution.py:265
  2032.0 29.0 %all-gather.57.cloned.1.call-done = bf16[768,768]{1,0:T(8,128)(2,1)} async-done(((bf16[192,768]{1,0:T(8,128)(2,1)}), bf16[768,768]{1,0:T(8,128)(2,1)}) %all-gather.57.cloned.1.call-update) | async-done | bytes 1179664 | tf_op jit(solution)/shard_map/all_gather | solution.py:271
  2094.5 29.4 %all-reduce.2 = f32[10752]{0:T(1024)} all-reduce(f32[10752]{0:T(1024)} %constant_dynamic-update-slice_fusion.10), channel_id=17, replica_groups=mesh['dp'=8,'own'=4] {'dp'}, use_global_device_ids=true, to_apply=%region_33.34.clone | all-reduce | flops 10752 | bytes 86016
  2186.0 26.8 %all-gather.89.cloned.1.call-done = bf16[768,768]{1,0:T(8,128)(2,1)} async-done(((bf16[192,768]{1,0:T(8,128)(2,1)}), bf16[768,768]{1,0:T(8,128)(2,1)}) %all-gather.89.cloned.1.call-update) | async-done | bytes 1179664 | tf_op jit(solution)/shard_map/all_gather | solution.py:280
  (615 shorter events, 1070.6 us)
Async XLA Ops:
  44.6 170.2 %all-gather.47.cloned.1.call-start = ((), (), s32[]{:S(2)}) async-start(), calls=%async_computation.13 | async-start | bytes 5308416 | tf_op jit(solution)/shard_map/all_gather | solution.py:206
  56.4 210.0 %all-gather.49.cloned.1.call-start = ((), (), s32[]{:S(2)}) async-start(), calls=%async_computation.14 | async-start | bytes 5308416 | tf_op jit(solution)/shard_map/all_gather | solution.py:207
  67.1 307.7 %reduce-scatter.19.cloned.1.call-start = ((), (), s32[]{:S(2)}) async-start(), calls=%async_computation.16 | async-start | bytes 2654208 | tf_op jit(solution)/shard_map/reduce_scatter | solution.py:216
  340.5 176.3 %reduce-scatter.21.cloned.1.call-start = ((), (), s32[]{:S(2)}) async-start(), calls=%async_computation.17 | async-start | bytes 10616832 | tf_op jit(solution)/shard_map/reduce_scatter | solution.py:217
  348.6 268.4 %reduce-scatter.25.cloned.1.call-start = ((), (), s32[]{:S(2)}) async-start(), calls=%async_computation.19 | async-start | bytes 10616832 | tf_op jit(solution)/shard_map/reduce_scatter | solution.py:218
  359.1 402.5 %reduce-scatter.29.cloned.1.call-start = ((), (), s32[]{:S(2)}) async-start(), calls=%async_computation.21 | async-start | bytes 15925248 | tf_op jit(solution)/shard_map/reduce_scatter | solution.py:219
  374.7 414.1 %reduce-scatter.33.cloned.1.call-start = ((), (), s32[]{:S(2)}) async-start(), calls=%async_computation.53 | async-start | bytes 491520
  376.7 444.2 %reduce-scatter.31.cloned.1.call-start = ((), (), s32[]{:S(2)}) async-start(), calls=%async_computation.52 | async-start | bytes 1474560
  419.1 434.0 %reduce-scatter.23.cloned.1.call-start = ((), (), s32[]{:S(2)}) async-start(), calls=%async_computation.18 | async-start | bytes 1474560 | tf_op jit(solution)/shard_map/reduce_scatter | solution.py:225
  516.8 368.5 %reduce-scatter.27.cloned.1.call-start = ((), (), s32[]{:S(2)}) async-start(), calls=%async_computation.20 | async-start | bytes 1474560 | tf_op jit(solution)/shard_map/reduce_scatter | solution.py:226
  617.0 305.9 %reduce-scatter.35.cloned.1.call-start = ((), (), s32[]{:S(2)}) async-start(), calls=%async_computation.54 | async-start | bytes 2457600
  764.5 311.9 %all-reduce.24.cloned.1.call-start = ((), (), s32[]{:S(2)}) async-start(), calls=%async_computation.59 | async-start | bytes 2359296 | tf_op jit(solution)/shard_map/psum | solution.py:265
  1078.3 151.6 %all-gather.101.cloned.1.call-start = ((), (), s32[]{:S(2)}) async-start(), calls=%async_computation.47 | async-start | bytes 2654208 | tf_op jit(solution)/shard_map/all_gather | solution.py:262
  1093.6 198.9 %all-reduce.22.cloned.1.call-start = ((), (), s32[]{:S(2)}) async-start(), calls=%async_computation.58 | async-start | bytes 2359296 | tf_op jit(solution)/shard_map/psum | solution.py:265
  1293.8 148.5 %all-gather.93.cloned.1.call-start = ((), (), s32[]{:S(2)}) async-start(), calls=%async_computation.43 | async-start | bytes 1474560 | tf_op jit(solution)/shard_map/all_gather | solution.py:283
  1294.4 181.6 %all-gather.103.cloned.1.call-start = ((), (), s32[]{:S(2)}) async-start(), calls=%async_computation.48 | async-start | bytes 2654208 | tf_op jit(solution)/shard_map/all_gather | solution.py:262
  1338.8 199.7 %all-reduce.20.cloned.1.call-start = ((), (), s32[]{:S(2)}) async-start(), calls=%async_computation.57 | async-start | bytes 2359296 | tf_op jit(solution)/shard_map/psum | solution.py:265
  1539.9 149.2 %all-gather.95.cloned.1.call-start = ((), (), s32[]{:S(2)}) async-start(), calls=%async_computation.44 | async-start | bytes 1474560 | tf_op jit(solution)/shard_map/all_gather | solution.py:283
  1540.6 182.1 %all-gather.105.cloned.1.call-start = ((), (), s32[]{:S(2)}) async-start(), calls=%async_computation.49 | async-start | bytes 2654208 | tf_op jit(solution)/shard_map/all_gather | solution.py:262
  1584.5 200.7 %all-reduce.18.cloned.1.call-start = ((), (), s32[]{:S(2)}) async-start(), calls=%async_computation.56 | async-start | bytes 2359296 | tf_op jit(solution)/shard_map/psum | solution.py:265
  1786.5 149.4 %all-gather.97.cloned.1.call-start = ((), (), s32[]{:S(2)}) async-start(), calls=%async_computation.45 | async-start | bytes 1474560 | tf_op jit(solution)/shard_map/all_gather | solution.py:283
  1787.2 182.3 %all-gather.107.cloned.1.call-start = ((), (), s32[]{:S(2)}) async-start(), calls=%async_computation.50 | async-start | bytes 2654208 | tf_op jit(solution)/shard_map/all_gather | solution.py:262
  1830.1 201.8 %all-reduce.16.cloned.1.call-start = ((), (), s32[]{:S(2)}) async-start(), calls=%async_computation.55 | async-start | bytes 2359296 | tf_op jit(solution)/shard_map/psum | solution.py:265
  1972.3 173.4 %all-gather.69.cloned.1.call-start = ((), (), s32[]{:S(2)}) async-start(), calls=%async_computation.31 | async-start | bytes 1474560 | tf_op jit(solution)/shard_map/all_gather | solution.py:274
  (160 other events, 7322.0 us)
Sparse Core Ops, SparseCore 0:
  24.2 71.8 all-gather.40
  98.2 40.0 all-gather.42
  163.7 51.0 all-gather.46
  216.3 50.0 all-gather.48
  294.6 35.5 reduce-scatter.18
  340.6 75.8 reduce-scatter.16
  418.8 97.8 reduce-scatter.20
  519.1 97.8 reduce-scatter.24
  619.1 142.4 reduce-scatter.28
  888.8 34.1 reduce-scatter.34
  1016.9 59.4 all-reduce.23
  1198.4 31.4 all-gather.100
  1233.1 59.3 all-reduce.21
  1413.1 29.1 all-gather.92
  1444.5 31.4 all-gather.102
  1479.2 59.3 all-reduce.19
  1628.9 29.1 all-gather.74
  1659.9 29.0 all-gather.94
  1691.3 31.4 all-gather.104
  1725.8 59.3 all-reduce.17
  1875.8 29.1 all-gather.76
  1938.1 31.4 all-gather.106
  1972.5 59.3 all-reduce.15
  2093.2 32.3 all-gather.108
  (26 shorter events, 712.7 us)
